TPU v7x, 32 devices: a whole 2x2x4 slice. The times are simulated.
32 devices in a mesh: dp: 2 (over y), seq: 16 (over z, x, core).
Axes of the slice: x: 2, y: 2, z: 4, core: 2. Of those that a mesh axis runs over, the one named last changes fastest.
Arguments:
- layer_input: bfloat16 [2, 2048, 1024], P('dp', 'seq'), may hold values from -12 to 12
- v_first: bfloat16 [2, 2048, 1024], P('dp', 'seq'), may hold values from -6 to 6
- cotangent: bfloat16 [2, 2048, 1024], P('dp', 'seq'), may hold values from -6 to 6
- segments: int32 [2, 2048], P('dp'), may hold values from 0 to 3, never falling along the last dimension, each value on 1 to 1024 neighbouring positions
- norm1_gain: bfloat16 [1024], P('seq'), may hold values from 0.099609375 to 1.8984375
- w_query: bfloat16 [1024, 1024], P('seq', 'dp'), may hold values from -0.1875 to 0.1875
- w_key: bfloat16 [1024, 1024], P('seq', 'dp'), may hold values from -0.1875 to 0.1875
- w_value: bfloat16 [1024, 1024], P('seq', 'dp'), may hold values from -0.1875 to 0.1875
- w_out: bfloat16 [1024, 1024], P('seq', 'dp'), may hold values from -1.5 to 1.5
- norm2_gain: bfloat16 [1024], P('seq'), may hold values from 0.099609375 to 1.8984375
- w_gate: bfloat16 [1024, 2816], P('seq', 'dp'), may hold values from -0.1875 to 0.1875
- w_up: bfloat16 [1024, 2816], P('seq', 'dp'), may hold values from -0.1875 to 0.1875
- w_down: bfloat16 [2816, 1024], P('seq', 'dp'), may hold values from -0.109375 to 0.109375
Outputs:
- out: bfloat16 [2, 2048, 1024], P('dp', 'seq')
- d_input: bfloat16 [2, 2048, 1024], P('dp', 'seq')
- d_v_first: bfloat16 [2, 2048, 1024], P('dp', 'seq')
- d_norm1_gain: float32 [1024], P('seq')
- d_w_query: float32 [1024, 1024], P('seq', 'dp')
- d_w_key: float32 [1024, 1024], P('seq', 'dp')
- d_w_value: float32 [1024, 1024], P('seq', 'dp')
- d_w_out: float32 [1024, 1024], P('seq', 'dp')
- d_norm2_gain: float32 [1024], P('seq')
- d_w_gate: float32 [1024, 2816], P('seq', 'dp')
- d_w_up: float32 [1024, 2816], P('seq', 'dp')
- d_w_down: float32 [2816, 1024], P('seq', 'dp')
- rms: float32 [3], replicated
Inputs may be any that keep to these rules, and one draw needn't show every extreme that they name: `segments`: in each row the ids start at 0 and never fall; every id up to 3 is used, by at most 1024 tokens.
All inputs are finite; a program needn't handle non-finite values.
Results may differ from a plain program's by a relative error of at most 0.022.
Values may be sent and summed in bfloat16 or wider, within the bound.
No kernel may reach another device: no remote copies, remote signals or barrier semaphores. Data moves between devices by JAX's collectives and lax.ppermute only.
A program may use at most 256 MiB of HBM per device.

v0:
```python
import jax
import jax.numpy as jnp
from jax import lax
from jax.sharding import PartitionSpec as P

H = 16
HS = 64
EPSILON = 1e-06


def normalize(rows_in, gain_in):
    return (
        rows_in * lax.rsqrt(jnp.mean(rows_in * rows_in, axis=-1, keepdims=True) + EPSILON) * gain_in
    )


def rotary_tables(positions):
    half_size = HS // 2
    frequency = 10000.0 ** (-jnp.arange(half_size, dtype=jnp.float32) * 2.0 / HS)
    angles = positions[..., None] * frequency
    return (jnp.cos(angles)[..., None, :], jnp.sin(angles)[..., None, :])


def rotate(values, cosine, sine_t):
    shaped = values.reshape(values.shape[:-1] + (H, HS))
    half_size = HS // 2
    lower_half = shaped[..., :half_size]
    upper_half = shaped[..., half_size:]
    turned = jnp.concatenate(
        [lower_half * cosine - upper_half * sine_t, upper_half * cosine + lower_half * sine_t],
        axis=-1,
    )
    return turned.reshape(values.shape)


def project(rows_in, weight):
    return jnp.einsum("sqi,ij->sqj", rows_in, weight, preferred_element_type=jnp.float32)


def project_back(grad_rows, weight):
    return jnp.einsum("sqj,ij->sqi", grad_rows, weight, preferred_element_type=jnp.float32)


def weight_grad(left_rows, right_rows):
    return jnp.einsum("sqi,sqj->ij", left_rows, right_rows, preferred_element_type=jnp.float32)


def fetch_forward(w_query, w_key, w_value, w_out, w_gate, w_up, w_down, norm1_gain, norm2_gain):
    wide_set = (
        lax.all_gather(w_query, "dp", axis=1, tiled=True),
        lax.all_gather(w_key, "dp", axis=1, tiled=True),
        lax.all_gather(w_value, "dp", axis=1, tiled=True),
        lax.all_gather(w_out, "dp", axis=1, tiled=True),
        lax.all_gather(w_gate, "dp", axis=1, tiled=True),
        lax.all_gather(w_up, "dp", axis=1, tiled=True),
        lax.all_gather(w_down, "dp", axis=1, tiled=True),
    )
    return (
        lax.all_gather(wide_set[0], "seq", axis=0, tiled=True),
        lax.all_gather(wide_set[1], "seq", axis=0, tiled=True),
        lax.all_gather(wide_set[2], "seq", axis=0, tiled=True),
        lax.all_gather(wide_set[3], "seq", axis=0, tiled=True),
        lax.all_gather(wide_set[4], "seq", axis=0, tiled=True),
        lax.all_gather(wide_set[5], "seq", axis=0, tiled=True),
        lax.all_gather(wide_set[6], "seq", axis=0, tiled=True),
        lax.all_gather(norm1_gain, "seq", axis=0, tiled=True),
        lax.all_gather(norm2_gain, "seq", axis=0, tiled=True),
    )


def fetch_backward(w_query, w_key, w_value, w_out, w_gate, w_up, w_down, norm1_gain, norm2_gain):
    wide_set = (
        lax.all_gather(w_query, "dp", axis=1, tiled=True),
        lax.all_gather(w_key, "dp", axis=1, tiled=True),
        lax.all_gather(w_value, "dp", axis=1, tiled=True),
        lax.all_gather(w_out, "dp", axis=1, tiled=True),
        lax.all_gather(w_gate, "dp", axis=1, tiled=True),
        lax.all_gather(w_up, "dp", axis=1, tiled=True),
        lax.all_gather(w_down, "dp", axis=1, tiled=True),
    )
    return (
        lax.all_gather(wide_set[0], "seq", axis=0, tiled=True),
        lax.all_gather(wide_set[1], "seq", axis=0, tiled=True),
        lax.all_gather(wide_set[2], "seq", axis=0, tiled=True),
        lax.all_gather(wide_set[3], "seq", axis=0, tiled=True),
        lax.all_gather(wide_set[4], "seq", axis=0, tiled=True),
        lax.all_gather(wide_set[5], "seq", axis=0, tiled=True),
        lax.all_gather(wide_set[6], "seq", axis=0, tiled=True),
        lax.all_gather(norm1_gain, "seq", axis=0, tiled=True),
        lax.all_gather(norm2_gain, "seq", axis=0, tiled=True),
    )


def local(
    layer_input,
    v_first,
    cotangent,
    segments,
    norm1_gain,
    w_query,
    w_key,
    w_value,
    w_out,
    norm2_gain,
    w_gate,
    w_up,
    w_down,
):
    num_seqs, own_tokens, model_width = layer_input.shape
    length = segments.shape[1]
    block_rows = min(1024, length)
    block_count = length // block_rows
    score_scale = HS ** (-0.5)
    offset = lax.axis_index("seq") * own_tokens
    own_seg = lax.dynamic_slice_in_dim(segments, offset, own_tokens, 1)
    own_index = offset + jnp.arange(own_tokens, dtype=jnp.int32)
    starts = jnp.sum((segments[:, None, :] < own_seg[:, :, None]).astype(jnp.int32), axis=2)
    cosine, sine_t = rotary_tables((own_index[None, :] - starts).astype(jnp.float32))
    block_ids = jnp.arange(block_count)
    full_set = fetch_forward(
        w_query, w_key, w_value, w_out, w_gate, w_up, w_down, norm1_gain, norm2_gain
    )
    input_f = layer_input.astype(jnp.float32)
    gain_one = full_set[7].astype(jnp.float32)
    gain_two = full_set[8].astype(jnp.float32)
    normed_one = normalize(input_f, gain_one).astype(jnp.bfloat16)
    query_raw = project(normed_one, full_set[0])
    key_raw = project(normed_one, full_set[1])
    mixed_values = (
        0.5 * project(normed_one, full_set[2]) + 0.5 * v_first.astype(jnp.float32)
    ).astype(jnp.bfloat16)
    q_rot = rotate(query_raw, cosine, sine_t).astype(jnp.bfloat16)
    k_rot = rotate(key_raw, cosine, sine_t).astype(jnp.bfloat16)
    keys_all, values_all = (
        lax.all_gather(k_rot, "seq", axis=1, tiled=True),
        lax.all_gather(mixed_values, "seq", axis=1, tiled=True),
    )
    keys_h = keys_all.reshape(num_seqs, length, H, HS)
    values_h = values_all.reshape(num_seqs, length, H, HS)
    query_h = q_rot.reshape(num_seqs, own_tokens, H, HS)

    def masked_scores(block_no):
        first_row = block_no * block_rows
        key_block = lax.dynamic_slice_in_dim(keys_h, first_row, block_rows, 1)
        value_block = lax.dynamic_slice_in_dim(values_h, first_row, block_rows, 1)
        seg_block = lax.dynamic_slice_in_dim(segments, first_row, block_rows, 1)
        key_index = first_row + jnp.arange(block_rows, dtype=jnp.int32)
        raw_scores = (
            jnp.einsum("sqhd,skhd->shqk", query_h, key_block, preferred_element_type=jnp.float32)
            * score_scale
        )
        allowed = (seg_block[:, None, :] == own_seg[:, :, None]) & (
            key_index[None, None, :] <= own_index[None, :, None]
        )
        return (jnp.where(allowed[:, None], raw_scores, -1e30), key_block, value_block)

    def lse_step(carried, block_no):
        running_max, running_sum = carried
        scores, _, _ = masked_scores(block_no)
        new_max = jnp.maximum(running_max, jnp.max(scores, axis=-1))
        running_sum = running_sum * jnp.exp(running_max - new_max) + jnp.sum(
            jnp.exp(scores - new_max[..., None]), axis=-1
        )
        return ((new_max, running_sum), None)

    stat_shape = (num_seqs, H, own_tokens)
    (running_max, running_sum), _ = lax.scan(
        lse_step,
        (jnp.full(stat_shape, -1e30, jnp.float32), jnp.zeros(stat_shape, jnp.float32)),
        block_ids,
    )
    log_total = running_max + jnp.log(running_sum)

    def attend_step(carried, block_no):
        scores, _, value_block = masked_scores(block_no)
        soft_b = jnp.exp(scores - log_total[..., None]).astype(jnp.bfloat16)
        return (
            carried
            + jnp.einsum(
                "shqk,skhd->sqhd", soft_b, value_block, preferred_element_type=jnp.float32
            ),
            None,
        )

    head_zeros = jnp.zeros((num_seqs, own_tokens, H, HS), jnp.float32)
    attended_f, _ = lax.scan(attend_step, head_zeros, block_ids)
    attended = attended_f.reshape(num_seqs, own_tokens, H * HS).astype(jnp.bfloat16)
    branch_a = project(attended, full_set[3])
    hidden_in = input_f + branch_a
    normed_two = normalize(hidden_in, gain_two).astype(jnp.bfloat16)
    gate_pre = project(normed_two, full_set[4])
    upward = project(normed_two, full_set[5])
    activated = (jax.nn.silu(gate_pre) * upward).astype(jnp.bfloat16)
    branch_m = project(activated, full_set[6])
    result = hidden_in + branch_m
    squares = jnp.stack(
        [jnp.sum(result * result), jnp.sum(branch_a * branch_a), jnp.sum(branch_m * branch_m)]
    )
    reused = fetch_backward(
        w_query, w_key, w_value, w_out, w_gate, w_up, w_down, norm1_gain, norm2_gain
    )
    grad_down = weight_grad(activated, cotangent)
    d_activated = project_back(cotangent, reused[6])
    gate_pull = jax.vjp(lambda gate_in, up_in: jax.nn.silu(gate_in) * up_in, gate_pre, upward)[1]
    d_gate_f, d_upward_f = gate_pull(d_activated)
    d_gate = d_gate_f.astype(jnp.bfloat16)
    d_upward = d_upward_f.astype(jnp.bfloat16)
    grad_gate = weight_grad(normed_two, d_gate)
    grad_up = weight_grad(normed_two, d_upward)
    d_normed_two = project_back(d_gate, reused[4]) + project_back(d_upward, reused[5])
    norm_pull_two = jax.vjp(normalize, hidden_in, gain_two)[1]
    d_hidden_part, d_gain_two = norm_pull_two(d_normed_two)
    d_hidden = cotangent.astype(jnp.float32) + d_hidden_part
    d_branch_a = d_hidden.astype(jnp.bfloat16)
    grad_out = weight_grad(attended, d_branch_a)
    d_attended = project_back(d_branch_a, reused[3]).astype(jnp.bfloat16)
    grad_h = d_attended.reshape(num_seqs, own_tokens, H, HS)

    def delta_step(carried, block_no):
        scores, _, value_block = masked_scores(block_no)
        soft_weights = jnp.exp(scores - log_total[..., None])
        d_soft = jnp.einsum(
            "sqhd,skhd->shqk", grad_h, value_block, preferred_element_type=jnp.float32
        )
        return (carried + jnp.sum(soft_weights * d_soft, axis=-1), None)

    row_delta, _ = lax.scan(delta_step, jnp.zeros(stat_shape, jnp.float32), block_ids)

    def score_grads(block_no):
        scores, key_block, value_block = masked_scores(block_no)
        soft_weights = jnp.exp(scores - log_total[..., None])
        d_soft = jnp.einsum(
            "sqhd,skhd->shqk", grad_h, value_block, preferred_element_type=jnp.float32
        )
        d_scores = (soft_weights * (d_soft - row_delta[..., None])).astype(jnp.bfloat16)
        return (soft_weights.astype(jnp.bfloat16), d_scores, key_block)

    def query_and_key(carried, block_no):
        soft_b, d_scores, key_block = score_grads(block_no)
        carried = carried + jnp.einsum(
            "shqk,skhd->sqhd", d_scores, key_block, preferred_element_type=jnp.float32
        )
        d_key_part = (
            jnp.einsum("shqk,sqhd->skhd", d_scores, query_h, preferred_element_type=jnp.float32)
            * score_scale
        )
        d_value_part = jnp.einsum(
            "shqk,sqhd->skhd", soft_b, grad_h, preferred_element_type=jnp.float32
        )
        return (carried, (d_key_part, d_value_part))

    d_query_h, (key_parts, value_parts) = lax.scan(query_and_key, head_zeros, block_ids)
    key_terms = jnp.moveaxis(key_parts, 0, 1).reshape(num_seqs, length, H * HS)
    value_terms = jnp.moveaxis(value_parts, 0, 1).reshape(num_seqs, length, H * HS)
    d_key_own, d_value_own = (
        lax.psum_scatter(
            key_terms.astype(jnp.bfloat16), "seq", scatter_dimension=1, tiled=True
        ).astype(jnp.float32),
        lax.psum_scatter(
            value_terms.astype(jnp.bfloat16), "seq", scatter_dimension=1, tiled=True
        ).astype(jnp.float32),
    )
    d_query_rot = d_query_h.reshape(num_seqs, own_tokens, H * HS) * score_scale
    d_query = rotate(d_query_rot, cosine, -sine_t).astype(jnp.bfloat16)
    d_key = rotate(d_key_own, cosine, -sine_t).astype(jnp.bfloat16)
    d_value = (0.5 * d_value_own).astype(jnp.bfloat16)
    grad_query = weight_grad(normed_one, d_query)
    grad_key = weight_grad(normed_one, d_key)
    grad_value = weight_grad(normed_one, d_value)
    d_normed_one = (
        project_back(d_query, reused[0])
        + project_back(d_key, reused[1])
        + project_back(d_value, reused[2])
    )
    norm_pull_one = jax.vjp(normalize, input_f, gain_one)[1]
    d_input_part, d_gain_one = norm_pull_one(d_normed_one)
    d_input = (d_hidden + d_input_part).astype(jnp.bfloat16)
    owned = (
        lax.psum_scatter(
            grad_query.astype(jnp.bfloat16), "seq", scatter_dimension=0, tiled=True
        ).astype(jnp.float32),
        lax.psum_scatter(
            grad_key.astype(jnp.bfloat16), "seq", scatter_dimension=0, tiled=True
        ).astype(jnp.float32),
        lax.psum_scatter(
            grad_value.astype(jnp.bfloat16), "seq", scatter_dimension=0, tiled=True
        ).astype(jnp.float32),
        lax.psum_scatter(
            grad_out.astype(jnp.bfloat16), "seq", scatter_dimension=0, tiled=True
        ).astype(jnp.float32),
        lax.psum_scatter(
            grad_gate.astype(jnp.bfloat16), "seq", scatter_dimension=0, tiled=True
        ).astype(jnp.float32),
        lax.psum_scatter(
            grad_up.astype(jnp.bfloat16), "seq", scatter_dimension=0, tiled=True
        ).astype(jnp.float32),
        lax.psum_scatter(
            grad_down.astype(jnp.bfloat16), "seq", scatter_dimension=0, tiled=True
        ).astype(jnp.float32),
    )
    final_set = (
        lax.psum_scatter(
            owned[0].astype(jnp.bfloat16), "dp", scatter_dimension=1, tiled=True
        ).astype(jnp.float32),
        lax.psum_scatter(
            owned[1].astype(jnp.bfloat16), "dp", scatter_dimension=1, tiled=True
        ).astype(jnp.float32),
        lax.psum_scatter(
            owned[2].astype(jnp.bfloat16), "dp", scatter_dimension=1, tiled=True
        ).astype(jnp.float32),
        lax.psum_scatter(
            owned[3].astype(jnp.bfloat16), "dp", scatter_dimension=1, tiled=True
        ).astype(jnp.float32),
        lax.psum_scatter(
            owned[4].astype(jnp.bfloat16), "dp", scatter_dimension=1, tiled=True
        ).astype(jnp.float32),
        lax.psum_scatter(
            owned[5].astype(jnp.bfloat16), "dp", scatter_dimension=1, tiled=True
        ).astype(jnp.float32),
        lax.psum_scatter(
            owned[6].astype(jnp.bfloat16), "dp", scatter_dimension=1, tiled=True
        ).astype(jnp.float32),
    )
    square_sums, gain_sums = lax.psum((squares, jnp.stack([d_gain_one, d_gain_two])), ("dp", "seq"))
    cell_count = num_seqs * own_tokens * model_width * lax.axis_size("dp") * lax.axis_size("seq")
    root_mean = jnp.sqrt(square_sums / cell_count)
    share = model_width // lax.axis_size("seq")
    gain_grads = lax.dynamic_slice_in_dim(gain_sums, lax.axis_index("seq") * share, share, 1)
    return (
        result.astype(jnp.bfloat16),
        d_input,
        d_value,
        gain_grads[0],
        final_set[0],
        final_set[1],
        final_set[2],
        final_set[3],
        gain_grads[1],
        final_set[4],
        final_set[5],
        final_set[6],
        root_mean,
    )


def solution(mesh):
    in_specs = (
        P("dp", "seq", None),
        P("dp", "seq", None),
        P("dp", "seq", None),
        P("dp", None),
        P("seq"),
        P("seq", "dp"),
        P("seq", "dp"),
        P("seq", "dp"),
        P("seq", "dp"),
        P("seq"),
        P("seq", "dp"),
        P("seq", "dp"),
        P("seq", "dp"),
    )
    out_specs = (
        P("dp", "seq", None),
        P("dp", "seq", None),
        P("dp", "seq", None),
        P("seq"),
        P("seq", "dp"),
        P("seq", "dp"),
        P("seq", "dp"),
        P("seq", "dp"),
        P("seq"),
        P("seq", "dp"),
        P("seq", "dp"),
        P("seq", "dp"),
        P(),
    )
    return jax.shard_map(local, mesh=mesh, in_specs=in_specs, out_specs=out_specs, check_vma=False)
```

profile of v0, /device:TPU:0, one launch (start us, length us, event | category | flops | bytes accessed | tf_op | source)
XLA Modules:
  0.0 1275.8 jit_solution(10179041738339998207)
XLA Ops:
  30.1 31.1 %all-reduce.3 = (bf16[1024]{0:T(1024)(128)(2,1)S(1)}, bf16[1024]{0:T(1024)(128)(2,1)S(1)}) all-reduce(bf16[1024]{0:T(1024)(128)(2,1)S(1)} %dynamic-update-slice, bf16[1024]{0:T(1024)(128)(2,1)S(1)} %dynamic-update-slice.1), channel_id=1, replica_groups=mesh['dp'=2,'seq'=16] {'seq'}, use_global_device_ids=true, to_apply=%add | all-reduce | flops 2048 | bytes 8192
  66.4 33.0 %all-gather.14.cloned.1.call-done = bf16[1024,1024]{1,0:T(8,128)(2,1)} async-done(((bf16[64,1024]{1,0:T(8,128)(2,1)}), bf16[1024,1024]{1,0:T(8,128)(2,1)}) %all-gather.14.cloned.1.call-update) | async-done | bytes 2097168 | tf_op jit(solution)/shard_map/all_gather | solution.py:60
  102.3 39.5 %all-gather.18.cloned.1.call-done = bf16[1024,1024]{1,0:T(8,128)(2,1)} async-done(((bf16[64,1024]{1,0:T(8,128)(2,1)}), bf16[1024,1024]{1,0:T(8,128)(2,1)}) %all-gather.18.cloned.1.call-update) | async-done | bytes 2097168 | tf_op jit(solution)/shard_map/all_gather | solution.py:59
  174.5 19.0 %all-gather.12.cloned.1.call-done = bf16[1,2048,1024]{2,1,0:T(8,128)(2,1)} async-done(((bf16[1,128,1024]{2,1,0:T(8,128)(2,1)}), bf16[1,2048,1024]{2,1,0:T(8,128)(2,1)}) %all-gather.12.cloned.1.call-update) | async-done | bytes 4194320 | tf_op jit(solution)/shard_map/all_gather | solution.py:136
  200.0 47.1 %all-gather.16.cloned.1.call-done = bf16[1,2048,1024]{1,2,0:T(8,128)(2,1)} async-done(((bf16[1,128,1024]{1,2,0:T(8,128)(2,1)}), bf16[1,2048,1024]{1,2,0:T(8,128)(2,1)}) %all-gather.16.cloned.1.call-update) | async-done | bytes 4194320 | tf_op jit(solution)/shard_map/all_gather | solution.py:135
  247.1 13.8 %while.50 = (s32[]{:T(128)}, f32[1,16,128]{2,1,0:T(8,128)S(1)}, f32[1,16,128]{2,1,0:T(8,128)S(1)}, s32[2]{0:T(128)S(1)}, s32[1,2048]{1,0:T(1,128)S(1)}, /*index=...) while((s32[]{:T(128)}, f32[1,16,128]{2,1,0:T(8,128)S(1)}, ...), condition=%wide.region_5.6_spmd.clone, body=%wide.region_2.5_spmd.clone.sunk | while | flops 283520128 | bytes 19658456 | solution.py:167
  260.9 14.2 %while.51 = (s32[]{:T(128)}, f32[1,128,16,64]{1,3,2,0:T(8,128)S(1)}, s32[2]{0:T(128)S(1)}, bf16[1,2048,16,64]{1,3,2,0:T(8,128)(2,1)}, s32[1,2048]{1,0:T(1,128)S(...) while((s32[]{:T(128)}, ...), condition=%wide.region_7.8_spmd.clone, body=%wide.region_6.7_spmd.clone.sunk | while | flops 545916032 | bytes 5799132 | solution.py:186
  291.8 56.7 %all-gather.24.cloned.1.call-done = bf16[1024,2816]{1,0:T(8,128)(2,1)} async-done(((bf16[64,2816]{1,0:T(8,128)(2,1)}), bf16[1024,2816]{1,0:T(8,128)(2,1)}) %all-gather.24.cloned.1.call-update) | async-done | bytes 5767184 | tf_op jit(solution)/shard_map/all_gather | solution.py:64
  353.1 55.0 %all-gather.22.cloned.1.call-done = bf16[1024,2816]{1,0:T(8,128)(2,1)} async-done(((bf16[64,2816]{1,0:T(8,128)(2,1)}), bf16[1024,2816]{1,0:T(8,128)(2,1)}) %all-gather.22.cloned.1.call-update) | async-done | bytes 5767184 | tf_op jit(solution)/shard_map/all_gather | solution.py:63
  412.8 54.9 %all-gather.26.cloned.1.call-done = bf16[2816,1024]{1,0:T(8,128)(2,1)} async-done(((bf16[176,1024]{1,0:T(8,128)(2,1)}), bf16[2816,1024]{1,0:T(8,128)(2,1)}) %all-gather.26.cloned.1.call-update) | async-done | bytes 5767184 | tf_op jit(solution)/shard_map/all_gather | solution.py:65
  489.5 17.2 %while.52 = (s32[]{:T(128)}, f32[1,16,128]{2,1,0:T(8,128)}, s32[2]{0:T(128)S(1)}, s32[1,2048]{1,0:T(1,128)S(1)}, s32[1,128]{1,0:T(1,128)S(1)}, /*index=5*/bf16[1...) while((s32[]{:T(128)}, f32[1,16,128]{2,1,0:T(8,128)}, ...), condition=%wide.region_12.13_spmd.clone, body=%wide.region_10.12_spmd.clone.sunk | while | flops 547753088 | bytes 38696792 | solution.py:227
  506.8 36.4 %while.53 = (s32[]{:T(128)}, f32[1,128,16,64]{1,3,2,0:T(8,128)S(1)}, bf16[2,1,1024,16,64]{2,4,3,1,0:T(8,128)(2,1)}, bf16[2,1,1024,16,64]{2,4,3,1,0:T(8,128)(2,1)...) while((s32[]{:T(128)}, ...), condition=%wide.region_14.15_spmd.clone, body=%wide.region_13.14_spmd.clone.sunk | while | flops 1364853888 | bytes 122140600 | solution.py:252
  577.1 28.8 %reshape.1048 = bf16[1,2048,1024]{2,0,1:T(2,128)(2,1)} reshape(bf16[2,1,1024,16,64]{4,3,2,0,1:T(8,128)(2,1)} %copy.84) | data formatting | bytes 8388608
  627.8 15.2 %reduce-scatter.23.cloned.1.call-done = bf16[1,128,1024]{2,1,0:T(8,128)(2,1)} async-done(((bf16[1,2048,1024]{2,1,0:T(8,128)(2,1)}), bf16[1,128,1024]{2,1,0:T(8,128)(2,1)}) %reduce-scatter.23.cloned.1.call-update) | async-done | bytes 262160 | tf_op jit(solution)/shard_map/reduce_scatter | solution.py:259
  646.3 72.3 %reduce-scatter.49.cloned.1.call-done = bf16[128,1024]{1,0:T(8,128)(2,1)} async-done(((bf16[2048,1024]{1,0:T(8,128)(2,1)}), bf16[128,1024]{1,0:T(8,128)(2,1)}) %reduce-scatter.49.cloned.1.call-update) | async-done | bytes 262160
  725.1 77.9 %reduce-scatter.43.cloned.1.call-done = bf16[64,2816]{1,0:T(8,128)(2,1)} async-done(((bf16[1024,2816]{1,0:T(8,128)(2,1)}), bf16[64,2816]{1,0:T(8,128)(2,1)}) %reduce-scatter.43.cloned.1.call-update) | async-done | bytes 360464 | tf_op jit(solution)/shard_map/reduce_scatter | solution.py:294
  805.2 82.1 %reduce-scatter.41.cloned.1.call-done = bf16[64,2816]{1,0:T(8,128)(2,1)} async-done(((bf16[1024,2816]{1,0:T(8,128)(2,1)}), bf16[64,2816]{1,0:T(8,128)(2,1)}) %reduce-scatter.41.cloned.1.call-update) | async-done | bytes 360464 | tf_op jit(solution)/shard_map/reduce_scatter | solution.py:291
  903.8 80.5 %reduce-scatter.45.cloned.1.call-done = bf16[176,1024]{1,0:T(8,128)(2,1)} async-done(((bf16[2816,1024]{1,0:T(8,128)(2,1)}), bf16[176,1024]{1,0:T(8,128)(2,1)}) %reduce-scatter.45.cloned.1.call-update) | async-done | bytes 360464 | tf_op jit(solution)/shard_map/reduce_scatter | solution.py:297
  988.5 40.3 %all-reduce.2 = (f32[2,1024]{1,0:T(2,128)S(1)}, f32[3]{0:T(128)S(1)}) all-reduce(f32[2,1024]{1,0:T(2,128)S(1)} %pad_maximum_fusion.2, f32[3]{0:T(128)S(1)} %pad_maximum_fusion.3), channel_id=1, replica_groups=mesh['dp'=2,'seq'=16] {'dp','seq'}, use_global_device_ids=true, to_apply=%region_20.21 | all-reduce | flops 2051 | bytes 16408 | tf_op jit(solution)/shard_map/psum | solution.py:324
  1028.9 20.1 %reduce-scatter.33.cloned.1.call-done = bf16[64,1024]{1,0:T(8,128)(2,1)} async-done(((bf16[1024,1024]{1,0:T(8,128)(2,1)}), bf16[64,1024]{1,0:T(8,128)(2,1)}) %reduce-scatter.33.cloned.1.call-update) | async-done | bytes 131088 | tf_op jit(solution)/shard_map/reduce_scatter | solution.py:285
  1049.6 63.8 %reduce-scatter.29.cloned.1.call-done = bf16[64,1024]{1,0:T(8,128)(2,1)} async-done(((bf16[1024,1024]{1,0:T(8,128)(2,1)}), bf16[64,1024]{1,0:T(8,128)(2,1)}) %reduce-scatter.29.cloned.1.call-update) | async-done | bytes 131088 | tf_op jit(solution)/shard_map/reduce_scatter | solution.py:282
  1114.0 63.8 %reduce-scatter.25.cloned.1.call-done = bf16[64,1024]{1,0:T(8,128)(2,1)} async-done(((bf16[1024,1024]{1,0:T(8,128)(2,1)}), bf16[64,1024]{1,0:T(8,128)(2,1)}) %reduce-scatter.25.cloned.1.call-update) | async-done | bytes 131088 | tf_op jit(solution)/shard_map/reduce_scatter | solution.py:279
  1179.8 15.9 %reduce-scatter.53.cloned.1.call-done = bf16[1408,64]{1,0:T(8,128)(2,1)} async-done(((bf16[2816,64]{1,0:T(8,128)(2,1)}), bf16[1408,64]{1,0:T(8,128)(2,1)}) %reduce-scatter.53.cloned.1.call-update) | async-done | bytes 180240
  1197.6 17.2 %reduce-scatter.51.cloned.1.call-done = bf16[1408,64]{1,0:T(8,128)(2,1)} async-done(((bf16[2816,64]{1,0:T(8,128)(2,1)}), bf16[1408,64]{1,0:T(8,128)(2,1)}) %reduce-scatter.51.cloned.1.call-update) | async-done | bytes 180240
  (337 shorter events, 339.4 us)
Async XLA Ops:
  14.9 84.4 %all-gather.14.cloned.1.call-start = ((), (), s32[]{:S(2)}) async-start(), calls=%async_computation.18 | async-start | bytes 2228224 | tf_op jit(solution)/shard_map/all_gather | solution.py:60
  20.3 121.5 %all-gather.18.cloned.1.call-start = ((), (), s32[]{:S(2)}) async-start(), calls=%async_computation.20 | async-start | bytes 2228224 | tf_op jit(solution)/shard_map/all_gather | solution.py:59
  26.5 167.0 %all-gather.12.cloned.1.call-start = ((), (), s32[]{:S(2)}) async-start(), calls=%async_computation.17 | async-start | bytes 4456448 | tf_op jit(solution)/shard_map/all_gather | solution.py:136
  65.3 181.8 %all-gather.16.cloned.1.call-start = ((), (), s32[]{:S(2)}) async-start(), calls=%async_computation.19 | async-start | bytes 4456448 | tf_op jit(solution)/shard_map/all_gather | solution.py:135
  149.9 138.9 %all-gather.20.cloned.1.call-start = ((), (), s32[]{:S(2)}) async-start(), calls=%async_computation.21 | async-start | bytes 2228224 | tf_op jit(solution)/shard_map/all_gather | solution.py:62
  155.0 193.5 %all-gather.24.cloned.1.call-start = ((), (), s32[]{:S(2)}) async-start(), calls=%async_computation.23 | async-start | bytes 6127616 | tf_op jit(solution)/shard_map/all_gather | solution.py:64
  161.4 246.7 %all-gather.22.cloned.1.call-start = ((), (), s32[]{:S(2)}) async-start(), calls=%async_computation.22 | async-start | bytes 6127616 | tf_op jit(solution)/shard_map/all_gather | solution.py:63
  167.8 300.0 %all-gather.26.cloned.1.call-start = ((), (), s32[]{:S(2)}) async-start(), calls=%async_computation.24 | async-start | bytes 6127616 | tf_op jit(solution)/shard_map/all_gather | solution.py:65
  174.1 448.4 %reduce-scatter.37.cloned.1.call-start = ((), (), s32[]{:S(2)}) async-start(), calls=%async_computation.32 | async-start | bytes 2228224 | tf_op jit(solution)/shard_map/reduce_scatter | solution.py:288
  506.7 136.3 %reduce-scatter.23.cloned.1.call-start = ((), (), s32[]{:S(2)}) async-start(), calls=%async_computation.25 | async-start | bytes 4456448 | tf_op jit(solution)/shard_map/reduce_scatter | solution.py:259
  566.1 152.5 %reduce-scatter.49.cloned.1.call-start = ((), (), s32[]{:S(2)}) async-start(), calls=%async_computation.38 | async-start | bytes 4456448
  613.1 189.9 %reduce-scatter.43.cloned.1.call-start = ((), (), s32[]{:S(2)}) async-start(), calls=%async_computation.35 | async-start | bytes 6127616 | tf_op jit(solution)/shard_map/reduce_scatter | solution.py:294
  618.2 269.1 %reduce-scatter.41.cloned.1.call-start = ((), (), s32[]{:S(2)}) async-start(), calls=%async_computation.34 | async-start | bytes 6127616 | tf_op jit(solution)/shard_map/reduce_scatter | solution.py:291
  622.4 276.6 %reduce-scatter.39.cloned.1.call-start = ((), (), s32[]{:S(2)}) async-start(), calls=%async_computation.33 | async-start | bytes 196608 | tf_op jit(solution)/shard_map/reduce_scatter | solution.py:311
  623.0 361.2 %reduce-scatter.45.cloned.1.call-start = ((), (), s32[]{:S(2)}) async-start(), calls=%async_computation.36 | async-start | bytes 6127616 | tf_op jit(solution)/shard_map/reduce_scatter | solution.py:297
  627.8 421.2 %reduce-scatter.33.cloned.1.call-start = ((), (), s32[]{:S(2)}) async-start(), calls=%async_computation.30 | async-start | bytes 2228224 | tf_op jit(solution)/shard_map/reduce_scatter | solution.py:285
  646.2 467.1 %reduce-scatter.29.cloned.1.call-start = ((), (), s32[]{:S(2)}) async-start(), calls=%async_computation.28 | async-start | bytes 2228224 | tf_op jit(solution)/shard_map/reduce_scatter | solution.py:282
  722.8 455.1 %reduce-scatter.25.cloned.1.call-start = ((), (), s32[]{:S(2)}) async-start(), calls=%async_computation.26 | async-start | bytes 2228224 | tf_op jit(solution)/shard_map/reduce_scatter | solution.py:279
  725.0 470.7 %reduce-scatter.53.cloned.1.call-start = ((), (), s32[]{:S(2)}) async-start(), calls=%async_computation.40 | async-start | bytes 1081344
  805.1 409.6 %reduce-scatter.51.cloned.1.call-start = ((), (), s32[]{:S(2)}) async-start(), calls=%async_computation.39 | async-start | bytes 1081344
  889.5 340.4 %reduce-scatter.47.cloned.1.call-start = ((), (), s32[]{:S(2)}) async-start(), calls=%async_computation.37 | async-start | bytes 540672 | tf_op jit(solution)/shard_map/reduce_scatter | solution.py:320
  984.2 258.2 %reduce-scatter.35.cloned.1.call-start = ((), (), s32[]{:S(2)}) async-start(), calls=%async_computation.31 | async-start | bytes 196608 | tf_op jit(solution)/shard_map/reduce_scatter | solution.py:308
  1049.0 206.0 %reduce-scatter.31.cloned.1.call-start = ((), (), s32[]{:S(2)}) async-start(), calls=%async_computation.29 | async-start | bytes 196608 | tf_op jit(solution)/shard_map/reduce_scatter | solution.py:305
  1113.4 154.2 %reduce-scatter.27.cloned.1.call-start = ((), (), s32[]{:S(2)}) async-start(), calls=%async_computation.27 | async-start | bytes 196608 | tf_op jit(solution)/shard_map/reduce_scatter | solution.py:302
  (58 other events, 2226.7 us)
Sparse Core Ops, SparseCore 0:
  15.1 42.0 all-gather.9
  59.3 39.9 all-gather.13
  101.5 40.1 all-gather.17
  144.3 49.0 all-gather.11
  196.0 51.0 all-gather.15
  249.1 39.6 all-gather.19
  291.1 57.3 all-gather.23
  350.7 57.2 all-gather.21
  410.4 57.2 all-gather.25
  506.8 60.4 reduce-scatter.36
  571.2 71.7 reduce-scatter.22
  646.7 71.8 reduce-scatter.48
  722.5 80.4 reduce-scatter.42
  806.7 80.5 reduce-scatter.40
  902.8 81.3 reduce-scatter.44
  987.8 61.1 reduce-scatter.32
  1052.6 60.7 reduce-scatter.28
  1117.1 60.6 reduce-scatter.24
  1179.9 15.7 reduce-scatter.52
  1197.9 16.7 reduce-scatter.50
  1217.0 12.8 reduce-scatter.46
  1232.1 10.3 reduce-scatter.34
  1244.5 10.3 reduce-scatter.30
  1257.1 10.3 reduce-scatter.26
  (1 shorter events, 9.6 us)
where the time goes:
time: 1280 us
  waiting for transfers between devices  880 us (69%)
  matrix products  120 us (9%)
  blocking collectives  114 us (9%)
  local copies, waits for them, and re-layouts  111 us (9%)
  other arithmetic  26.5 us (2%)
  between operations  15.6 us (1%)
    unnamed x28, waiting for transfers between devices  106 us
    reduce_scatter x1, waiting for transfers between devices, local(): lax.psum_scatter(grad_gate.astype(jnp.bfloat16), 'seq', scatter_dimension...  82.1 us
    reduce_scatter x1, waiting for transfers between devices, local(): lax.psum_scatter(grad_down.astype(jnp.bfloat16), 'seq', scatter_dimension...  80.5 us
    reduce_scatter x1, waiting for transfers between devices, local(): lax.psum_scatter(grad_up.astype(jnp.bfloat16), 'seq', scatter_dimension=0...  77.9 us
    reduce_scatter x1, waiting for transfers between devices, local(): lax.psum_scatter(grad_query.astype(jnp.bfloat16), 'seq', scatter_dimensio...  63.8 us
    reduce_scatter x1, waiting for transfers between devices, local(): lax.psum_scatter(grad_key.astype(jnp.bfloat16), 'seq', scatter_dimension=...  63.8 us
    unnamed x88, local copies, waits for them, and re-layouts  60.8 us
    all_gather x1, waiting for transfers between devices, fetch_forward(): lax.all_gather(wide_set[5], 'seq', axis=0, tiled=True)  56.7 us
  transfers between devices with their start and end apart: 25, of which 23 were waited for; matrix products, arithmetic and copies ran while one was open for 17% of the time, Pallas kernels for 0%

commit v1 on v0

--- a/solution.py
+++ b/solution.py
@@ -6,6 +6,18 @@
 H = 16
 HS = 64
 EPSILON = 1e-06
+
+
+def doubled_up(shard, axis, dim):
+    ways, here = (lax.axis_size(axis), lax.axis_index(axis))
+    grown, reach = (shard, 1)
+    while reach < ways:
+        theirs = lax.ppermute(grown, axis, [(d, d ^ reach) for d in range(ways)])
+        mine_first = jnp.concatenate([grown, theirs], axis=dim)
+        theirs_first = jnp.concatenate([theirs, grown], axis=dim)
+        grown = jnp.where(here & reach == 0, mine_first, theirs_first)
+        reach = 2 * reach
+    return grown
 
 
 def normalize(rows_in, gain_in):
@@ -60,7 +72,7 @@
         lax.all_gather(wide_set[1], "seq", axis=0, tiled=True),
         lax.all_gather(wide_set[2], "seq", axis=0, tiled=True),
         lax.all_gather(wide_set[3], "seq", axis=0, tiled=True),
-        lax.all_gather(wide_set[4], "seq", axis=0, tiled=True),
+        doubled_up(wide_set[4], "seq", 0),
         lax.all_gather(wide_set[5], "seq", axis=0, tiled=True),
         lax.all_gather(wide_set[6], "seq", axis=0, tiled=True),
         lax.all_gather(norm1_gain, "seq", axis=0, tiled=True),

time: 1280 us -> 1410 us (1.10)
  waiting for transfers between devices: 880 us -> 976 us
  matrix products: 120 us -> 143 us
    ppermute x0 -> x4, waiting for transfers between devices: none -> 80.2 us  [doubled_up(): theirs = lax.ppermute(grown, axis, [(d, d ^ reach) for d in range(ways)])]
    all_gather x1, waiting for transfers between devices: 19 us -> 85.6 us  [local(): lax.all_gather(mixed_values, 'seq', axis=1, tiled=True)]
    all_gather x1, waiting for transfers between devices: 54.9 us -> 0.02 us  [fetch_forward(): lax.all_gather(wide_set[6], 'seq', axis=0, tiled=True)]
    reduce_scatter x1, waiting for transfers between devices: 15.2 us -> 69.1 us  [local(): lax.psum_scatter(value_terms.astype(jnp.bfloat16), 'seq', scatter_dimensi...]
    reduce_scatter x1, waiting for transfers between devices: 20.1 us -> 63.8 us  [local(): lax.psum_scatter(grad_value.astype(jnp.bfloat16), 'seq', scatter_dimensio...]
    reduce_scatter x1, waiting for transfers between devices: 63.8 us -> 20.1 us  [local(): lax.psum_scatter(grad_query.astype(jnp.bfloat16), 'seq', scatter_dimensio...]
    unnamed x28, waiting for transfers between devices: 106 us -> 67.2 us
    unnamed x88 -> x80, local copies, waits for them, and re-layouts: 60.8 us -> 60.8 us
  transfers between devices with their start and end apart: 25 -> 29, of which waited for: 23 -> 25; matrix products, arithmetic and copies ran while one was open for 17% -> 18% of each run, Pallas kernels for 0% -> 0%
where the time goes in v1:
time: 1410 us; the launch traced here: 1400 us
  waiting for transfers between devices  976 us (69%)
  matrix products  143 us (10%)
  blocking collectives  114 us (8%)
  local copies, waits for them, and re-layouts  107 us (8%)
  other arithmetic  39.2 us (3%)
  between operations  15.6 us (1%)
    all_gather x1, waiting for transfers between devices, local(): lax.all_gather(mixed_values, 'seq', axis=1, tiled=True)  85.6 us
    reduce_scatter x1, waiting for transfers between devices, local(): lax.psum_scatter(grad_up.astype(jnp.bfloat16), 'seq', scatter_dimension=0...  82.2 us
    reduce_scatter x1, waiting for transfers between devices, local(): lax.psum_scatter(grad_gate.astype(jnp.bfloat16), 'seq', scatter_dimension...  81.1 us
    reduce_scatter x1, waiting for transfers between devices, local(): lax.psum_scatter(grad_down.astype(jnp.bfloat16), 'seq', scatter_dimension...  80.4 us
    ppermute x4, waiting for transfers between devices, doubled_up(): theirs = lax.ppermute(grown, axis, [(d, d ^ reach) for d in range(ways)])  80.2 us
    reduce_scatter x1, waiting for transfers between devices, local(): lax.psum_scatter(value_terms.astype(jnp.bfloat16), 'seq', scatter_dimensi...  69.1 us
    unnamed x28, waiting for transfers between devices  67.2 us
    reduce_scatter x1, waiting for transfers between devices, local(): lax.psum_scatter(grad_value.astype(jnp.bfloat16), 'seq', scatter_dimensio...  63.8 us
  transfers between devices with their start and end apart: 29, of which 25 were waited for; matrix products, arithmetic and copies ran while one was open for 18% of the time, Pallas kernels for 0%

profile of v1, /device:TPU:0, one launch (start us, length us, event | category | flops | bytes accessed | tf_op | source)
XLA Modules:
  0.0 1402.8 jit_solution(1529408263581037334)
XLA Ops:
  36.7 30.5 %all-reduce.3 = (bf16[1024]{0:T(1024)(128)(2,1)S(1)}, bf16[1024]{0:T(1024)(128)(2,1)S(1)}) all-reduce(bf16[1024]{0:T(1024)(128)(2,1)S(1)} %dynamic-update-slice, bf16[1024]{0:T(1024)(128)(2,1)S(1)} %dynamic-update-slice.1), channel_id=1, replica_groups=mesh['dp'=2,'seq'=16] {'seq'}, use_global_device_ids=true, to_apply=%add | all-reduce | flops 2048 | bytes 8192
  72.4 26.9 %all-gather.18.cloned.1.call-done = bf16[1024,1024]{1,0:T(8,128)(2,1)} async-done(((bf16[64,1024]{1,0:T(8,128)(2,1)}), bf16[1024,1024]{1,0:T(8,128)(2,1)}) %all-gather.18.cloned.1.call-update) | async-done | bytes 2097168 | tf_op jit(solution)/shard_map/all_gather | solution.py:71
  102.2 39.5 %all-gather.14.cloned.1.call-done = bf16[1024,1024]{1,0:T(8,128)(2,1)} async-done(((bf16[64,1024]{1,0:T(8,128)(2,1)}), bf16[1024,1024]{1,0:T(8,128)(2,1)}) %all-gather.14.cloned.1.call-update) | async-done | bytes 2097168 | tf_op jit(solution)/shard_map/all_gather | solution.py:72
  170.5 32.8 %collective-permute-done.1 = bf16[128,2816]{1,0:T(8,128)(2,1)} collective-permute-done((bf16[128,2816]{1,0:T(8,128)(2,1)S(1)}, bf16[128,2816]{1,0:T(8,128)(2,1)}, u32[]{:S(2)}, u32[]{:S(2)}) %collective-permute-start.1) | collective-permute-done | bytes 720928 | tf_op jit(solution)/shard_map/ppermute | solution.py:15
  206.0 45.7 %collective-permute-done.2 = bf16[256,2816]{1,0:T(8,128)(2,1)} collective-permute-done((bf16[256,2816]{1,0:T(8,128)(2,1)S(1)}, bf16[256,2816]{1,0:T(8,128)(2,1)}, u32[]{:S(2)}, u32[]{:S(2)}) %collective-permute-start.2) | collective-permute-done | bytes 1441824 | tf_op jit(solution)/shard_map/ppermute | solution.py:15
  260.9 85.6 %all-gather.12.cloned.1.call-done = bf16[1,2048,1024]{2,1,0:T(8,128)(2,1)} async-done(((bf16[1,128,1024]{2,1,0:T(8,128)(2,1)}), bf16[1,2048,1024]{2,1,0:T(8,128)(2,1)}) %all-gather.12.cloned.1.call-update) | async-done | bytes 4194320 | tf_op jit(solution)/shard_map/all_gather | solution.py:148
  353.0 58.0 %all-gather.16.cloned.1.call-done = bf16[1,2048,1024]{1,2,0:T(8,128)(2,1)} async-done(((bf16[1,128,1024]{1,2,0:T(8,128)(2,1)}), bf16[1,2048,1024]{1,2,0:T(8,128)(2,1)}) %all-gather.16.cloned.1.call-update) | async-done | bytes 4194320 | tf_op jit(solution)/shard_map/all_gather | solution.py:147
  410.9 26.9 %while.50 = (s32[]{:T(128)}, f32[1,16,128]{2,1,0:T(8,128)S(1)}, f32[1,16,128]{2,1,0:T(8,128)S(1)}, s32[2]{0:T(128)S(1)}, s32[1,2048]{1,0:T(1,128)S(1)}, /*index=...) while((s32[]{:T(128)}, f32[1,16,128]{2,1,0:T(8,128)S(1)}, ...), condition=%wide.region_5.6_spmd.clone, body=%wide.region_2.5_spmd.clone.sunk | while | flops 283520128 | bytes 19658448 | solution.py:179
  457.1 56.7 %all-gather.22.cloned.1.call-done = bf16[1024,2816]{1,0:T(8,128)(2,1)} async-done(((bf16[64,2816]{1,0:T(8,128)(2,1)}), bf16[1024,2816]{1,0:T(8,128)(2,1)}) %all-gather.22.cloned.1.call-update) | async-done | bytes 5767184 | tf_op jit(solution)/shard_map/all_gather | solution.py:76
  526.9 47.1 %all-gather.26.cloned.1.call-done = bf16[1024,2816]{1,0:T(8,128)(2,1)} async-done(((bf16[64,2816]{1,0:T(8,128)(2,1)}), bf16[1024,2816]{1,0:T(8,128)(2,1)}) %all-gather.26.cloned.1.call-update) | async-done | bytes 5767184 | tf_op jit(solution)/shard_map/all_gather | solution.py:98
  586.9 16.0 %while.52 = (s32[]{:T(128)}, f32[1,16,128]{2,1,0:T(8,128)S(1)}, s32[2]{0:T(128)S(1)}, s32[1,2048]{1,0:T(1,128)S(1)}, s32[1,128]{1,0:T(1,128)S(1)}, /*index=5*/bf...) while((s32[]{:T(128)}, f32[1,16,128]{2,1,0:T(8,128)S(1)}, ...), condition=%wide.region_12.13_spmd.clone, body=%wide.region_10.12_spmd.clone.sunk | while | flops 547753088 | bytes 38598400 | solution.py:239
  603.0 48.4 %while.53 = (s32[]{:T(128)}, f32[1,128,16,64]{1,3,2,0:T(8,128)S(1)}, bf16[2,1,1024,16,64]{2,4,3,1,0:T(8,128)(2,1)}, bf16[2,1,1024,16,64]{2,4,3,1,0:T(8,128)(2,1)...) while((s32[]{:T(128)}, ...), condition=%wide.region_14.15_spmd.clone, body=%wide.region_13.14_spmd.clone.sunk | while | flops 1364853888 | bytes 122075984 | solution.py:264
  662.4 28.6 %reshape.1048 = bf16[1,2048,1024]{2,0,1:T(2,128)(2,1)} reshape(bf16[2,1,1024,16,64]{4,3,2,0,1:T(8,128)(2,1)} %copy.84) | data formatting | bytes 8388608
  736.7 33.2 %reduce-scatter.49.cloned.1.call-done = bf16[128,1024]{1,0:T(8,128)(2,1)} async-done(((bf16[2048,1024]{1,0:T(8,128)(2,1)}), bf16[128,1024]{1,0:T(8,128)(2,1)}) %reduce-scatter.49.cloned.1.call-update) | async-done | bytes 262160
  776.4 69.1 %reduce-scatter.23.cloned.1.call-done = bf16[1,128,1024]{2,1,0:T(8,128)(2,1)} async-done(((bf16[1,2048,1024]{2,1,0:T(8,128)(2,1)}), bf16[1,128,1024]{2,1,0:T(8,128)(2,1)}) %reduce-scatter.23.cloned.1.call-update) | async-done | bytes 262160 | tf_op jit(solution)/shard_map/reduce_scatter | solution.py:271
  848.7 81.1 %reduce-scatter.41.cloned.1.call-done = bf16[64,2816]{1,0:T(8,128)(2,1)} async-done(((bf16[1024,2816]{1,0:T(8,128)(2,1)}), bf16[64,2816]{1,0:T(8,128)(2,1)}) %reduce-scatter.41.cloned.1.call-update) | async-done | bytes 360464 | tf_op jit(solution)/shard_map/reduce_scatter | solution.py:303
  932.0 82.2 %reduce-scatter.43.cloned.1.call-done = bf16[64,2816]{1,0:T(8,128)(2,1)} async-done(((bf16[1024,2816]{1,0:T(8,128)(2,1)}), bf16[64,2816]{1,0:T(8,128)(2,1)}) %reduce-scatter.43.cloned.1.call-update) | async-done | bytes 360464 | tf_op jit(solution)/shard_map/reduce_scatter | solution.py:306
  1030.7 80.4 %reduce-scatter.45.cloned.1.call-done = bf16[176,1024]{1,0:T(8,128)(2,1)} async-done(((bf16[2816,1024]{1,0:T(8,128)(2,1)}), bf16[176,1024]{1,0:T(8,128)(2,1)}) %reduce-scatter.45.cloned.1.call-update) | async-done | bytes 360464 | tf_op jit(solution)/shard_map/reduce_scatter | solution.py:309
  1115.5 40.3 %all-reduce.2 = (f32[2,1024]{1,0:T(2,128)S(1)}, f32[3]{0:T(128)S(1)}) all-reduce(f32[2,1024]{1,0:T(2,128)S(1)} %pad_maximum_fusion.2, f32[3]{0:T(128)S(1)} %pad_maximum_fusion.3), channel_id=1, replica_groups=mesh['dp'=2,'seq'=16] {'dp','seq'}, use_global_device_ids=true, to_apply=%region_20.21 | all-reduce | flops 2051 | bytes 16408 | tf_op jit(solution)/shard_map/psum | solution.py:336
  1155.8 20.1 %reduce-scatter.25.cloned.1.call-done = bf16[64,1024]{1,0:T(8,128)(2,1)} async-done(((bf16[1024,1024]{1,0:T(8,128)(2,1)}), bf16[64,1024]{1,0:T(8,128)(2,1)}) %reduce-scatter.25.cloned.1.call-update) | async-done | bytes 131088 | tf_op jit(solution)/shard_map/reduce_scatter | solution.py:291
  1176.6 63.8 %reduce-scatter.29.cloned.1.call-done = bf16[64,1024]{1,0:T(8,128)(2,1)} async-done(((bf16[1024,1024]{1,0:T(8,128)(2,1)}), bf16[64,1024]{1,0:T(8,128)(2,1)}) %reduce-scatter.29.cloned.1.call-update) | async-done | bytes 131088 | tf_op jit(solution)/shard_map/reduce_scatter | solution.py:294
  1241.0 63.8 %reduce-scatter.33.cloned.1.call-done = bf16[64,1024]{1,0:T(8,128)(2,1)} async-done(((bf16[1024,1024]{1,0:T(8,128)(2,1)}), bf16[64,1024]{1,0:T(8,128)(2,1)}) %reduce-scatter.33.cloned.1.call-update) | async-done | bytes 131088 | tf_op jit(solution)/shard_map/reduce_scatter | solution.py:297
  1306.8 15.9 %reduce-scatter.51.cloned.1.call-done = bf16[1408,64]{1,0:T(8,128)(2,1)} async-done(((bf16[2816,64]{1,0:T(8,128)(2,1)}), bf16[1408,64]{1,0:T(8,128)(2,1)}) %reduce-scatter.51.cloned.1.call-update) | async-done | bytes 180240
  1324.6 17.2 %reduce-scatter.53.cloned.1.call-done = bf16[1408,64]{1,0:T(8,128)(2,1)} async-done(((bf16[2816,64]{1,0:T(8,128)(2,1)}), bf16[1408,64]{1,0:T(8,128)(2,1)}) %reduce-scatter.53.cloned.1.call-update) | async-done | bytes 180240
  (317 shorter events, 376.5 us)
Async XLA Ops:
  20.3 121.4 %all-gather.14.cloned.1.call-start = ((), (), s32[]{:S(2)}) async-start(), calls=%async_computation.18 | async-start | bytes 2228224 | tf_op jit(solution)/shard_map/all_gather | solution.py:72
  26.5 228.7 %all-gather.24.cloned.1.call-start = ((), (), s32[]{:S(2)}) async-start(), calls=%async_computation.23 | async-start | bytes 6127616 | tf_op jit(solution)/shard_map/all_gather | solution.py:77
  33.1 313.4 %all-gather.12.cloned.1.call-start = ((), (), s32[]{:S(2)}) async-start(), calls=%async_computation.17 | async-start | bytes 4456448 | tf_op jit(solution)/shard_map/all_gather | solution.py:148
  71.3 339.6 %all-gather.16.cloned.1.call-start = ((), (), s32[]{:S(2)}) async-start(), calls=%async_computation.19 | async-start | bytes 4456448 | tf_op jit(solution)/shard_map/all_gather | solution.py:147
  149.8 304.3 %all-gather.20.cloned.1.call-start = ((), (), s32[]{:S(2)}) async-start(), calls=%async_computation.21 | async-start | bytes 2228224 | tf_op jit(solution)/shard_map/all_gather | solution.py:74
  154.9 358.9 %all-gather.22.cloned.1.call-start = ((), (), s32[]{:S(2)}) async-start(), calls=%async_computation.22 | async-start | bytes 6127616 | tf_op jit(solution)/shard_map/all_gather | solution.py:76
  161.6 412.5 %all-gather.26.cloned.1.call-start = ((), (), s32[]{:S(2)}) async-start(), calls=%async_computation.24 | async-start | bytes 6127616 | tf_op jit(solution)/shard_map/all_gather | solution.py:98
  205.6 525.6 %reduce-scatter.37.cloned.1.call-start = ((), (), s32[]{:S(2)}) async-start(), calls=%async_computation.32 | async-start | bytes 2228224 | tf_op jit(solution)/shard_map/reduce_scatter | solution.py:300
  255.1 262.5 %collective-permute-start.3 = (bf16[512,2816]{1,0:T(8,128)(2,1)}, bf16[512,2816]{1,0:T(8,128)(2,1)}, u32[]{:S(2)}, u32[]{:S(2)}) collective-permute-start(bf16[512,2816]{1,0:T(8,128)(2,1)} %maximum_select_fusion.2), channel_id=1, source_target_pairs={{0,8},{1,9},{2,10},{3,11},{4,12},{5,13},{6,14},{7,15},{8,0},{9,1},... | collective-permute-start | bytes 8650760 | tf_op jit(solution)/shard_map/ppermute | solution.py:15
  602.9 166.9 %reduce-scatter.49.cloned.1.call-start = ((), (), s32[]{:S(2)}) async-start(), calls=%async_computation.38 | async-start | bytes 4456448
  698.1 147.4 %reduce-scatter.23.cloned.1.call-start = ((), (), s32[]{:S(2)}) async-start(), calls=%async_computation.25 | async-start | bytes 4456448 | tf_op jit(solution)/shard_map/reduce_scatter | solution.py:271
  721.3 208.5 %reduce-scatter.41.cloned.1.call-start = ((), (), s32[]{:S(2)}) async-start(), calls=%async_computation.34 | async-start | bytes 6127616 | tf_op jit(solution)/shard_map/reduce_scatter | solution.py:303
  725.7 288.6 %reduce-scatter.43.cloned.1.call-start = ((), (), s32[]{:S(2)}) async-start(), calls=%async_computation.35 | async-start | bytes 6127616 | tf_op jit(solution)/shard_map/reduce_scatter | solution.py:306
  731.2 294.8 %reduce-scatter.39.cloned.1.call-start = ((), (), s32[]{:S(2)}) async-start(), calls=%async_computation.33 | async-start | bytes 196608 | tf_op jit(solution)/shard_map/reduce_scatter | solution.py:323
  731.8 379.4 %reduce-scatter.45.cloned.1.call-start = ((), (), s32[]{:S(2)}) async-start(), calls=%async_computation.36 | async-start | bytes 6127616 | tf_op jit(solution)/shard_map/reduce_scatter | solution.py:309
  736.6 439.3 %reduce-scatter.25.cloned.1.call-start = ((), (), s32[]{:S(2)}) async-start(), calls=%async_computation.26 | async-start | bytes 2228224 | tf_op jit(solution)/shard_map/reduce_scatter | solution.py:291
  774.1 466.2 %reduce-scatter.29.cloned.1.call-start = ((), (), s32[]{:S(2)}) async-start(), calls=%async_computation.28 | async-start | bytes 2228224 | tf_op jit(solution)/shard_map/reduce_scatter | solution.py:294
  776.3 528.5 %reduce-scatter.33.cloned.1.call-start = ((), (), s32[]{:S(2)}) async-start(), calls=%async_computation.30 | async-start | bytes 2228224 | tf_op jit(solution)/shard_map/reduce_scatter | solution.py:297
  848.6 474.0 %reduce-scatter.51.cloned.1.call-start = ((), (), s32[]{:S(2)}) async-start(), calls=%async_computation.39 | async-start | bytes 1081344
  932.0 409.8 %reduce-scatter.53.cloned.1.call-start = ((), (), s32[]{:S(2)}) async-start(), calls=%async_computation.40 | async-start | bytes 1081344
  1016.4 340.5 %reduce-scatter.47.cloned.1.call-start = ((), (), s32[]{:S(2)}) async-start(), calls=%async_computation.37 | async-start | bytes 540672 | tf_op jit(solution)/shard_map/reduce_scatter | solution.py:332
  1111.2 258.3 %reduce-scatter.27.cloned.1.call-start = ((), (), s32[]{:S(2)}) async-start(), calls=%async_computation.27 | async-start | bytes 196608 | tf_op jit(solution)/shard_map/reduce_scatter | solution.py:314
  1176.0 206.0 %reduce-scatter.31.cloned.1.call-start = ((), (), s32[]{:S(2)}) async-start(), calls=%async_computation.29 | async-start | bytes 196608 | tf_op jit(solution)/shard_map/reduce_scatter | solution.py:317
  1240.3 154.2 %reduce-scatter.35.cloned.1.call-start = ((), (), s32[]{:S(2)}) async-start(), calls=%async_computation.31 | async-start | bytes 196608 | tf_op jit(solution)/shard_map/reduce_scatter | solution.py:320
  (46 other events, 1938.8 us)
Sparse Core Ops, SparseCore 0:
  15.1 41.9 all-gather.9
  59.2 40.0 all-gather.17
  101.4 40.1 all-gather.13
  143.8 75.3 all-gather.23
  221.8 124.6 all-gather.11
  349.1 61.7 all-gather.15
  413.1 40.9 all-gather.19
  456.3 57.4 all-gather.21
  516.7 57.2 all-gather.25
  603.1 60.4 reduce-scatter.36
  698.2 71.6 reduce-scatter.48
  773.6 71.8 reduce-scatter.22
  849.4 80.4 reduce-scatter.40
  933.6 80.6 reduce-scatter.42
  1029.7 81.3 reduce-scatter.44
  1114.8 61.1 reduce-scatter.24
  1179.5 60.7 reduce-scatter.28
  1244.0 60.7 reduce-scatter.32
  1306.9 15.7 reduce-scatter.50
  1324.9 16.7 reduce-scatter.52
  1344.0 12.8 reduce-scatter.46
  1359.1 10.3 reduce-scatter.26
  1371.6 10.3 reduce-scatter.30
  1384.2 10.3 reduce-scatter.34
  (1 shorter events, 9.6 us)
